TPU v7x, 32 devices: a whole 2x2x4 slice. The times are simulated.
32 devices in a mesh: member: 4 (over y, x), grid: 8 (over z, core).
Axes of the slice: x: 2, y: 2, z: 4, core: 2. Of those that a mesh axis runs over, the one named last changes fastest.
Arguments:
- latent: bfloat16 [4, 16384, 1024], P('member', 'grid'), may hold values from -6 to 6
- w_in: bfloat16 [1024, 1024], P(('member', 'grid')), may hold values from -0.1875 to 0.1875
- b_in: float32 [1024], replicated, may hold values from -3 to 3
- w_out: bfloat16 [100, 1024], replicated, may hold values from -0.1875 to 0.1875
- b_out: float32 [100], replicated, may hold values from -3 to 3
- targets: float32 [100, 16384], P(None, 'grid'), may hold values from -6 to 6
- var_weight: float32 [100], replicated, may hold values from 0.5 to 5
- plan: int32 [3, 4], replicated, may hold values from 0 to 3, as said below
Outputs:
- loss: float32 [], replicated
- grad_latent: bfloat16 [4, 16384, 1024], P('member', 'grid')
- grad_w_in: float32 [1024, 1024], P(('member', 'grid'))
- grad_b_in: float32 [1024], replicated
- grad_w_out: float32 [100, 1024], replicated
- grad_b_out: float32 [100], replicated
Inputs may be any that keep to these rules, and one draw needn't show every extreme that they name: `plan`: each row is a perfect pairing of the 4 members: no member is its own partner, the partner of a member's partner is the member, and no pair occurs in two rows.
All inputs are finite; a program needn't handle non-finite values.
Results may differ from a plain program's by a relative error of at most 0.0095.
Values may be sent and summed in bfloat16 or wider, within the bound.
A program may use at most 128 MiB of HBM per device.

v0:
```python
import jax
import jax.numpy as jnp
from jax import lax
from jax.sharding import PartitionSpec as P

DELTA = 0.25


def make_fold(mine, partner_rows):

    def fold(carry, piece, start):
        count = piece.shape[0]
        labels = jnp.arange(count, dtype=jnp.int32)
        weights = jnp.sum((partner_rows[:, None] == labels[None, :]).astype(jnp.float32), axis=0)
        diff = mine[None] - piece
        root = jnp.sqrt(diff * diff + DELTA * DELTA)
        slope_sum = jnp.einsum("k,kvp->vp", weights, diff / root)
        spread_sum = jnp.einsum("k,kvp->vp", weights, root - DELTA)
        return (slope_sum, spread_sum)

    return fold


def shards(latent, w_in, b_in, w_out, b_out, targets, var_weight, plan):
    hidden_in = latent[0]
    points = hidden_in.shape[0]
    rounds = plan.shape[0]
    w_full = lax.all_gather(w_in, ("member", "grid"), axis=0, tiled=True)
    member = lax.axis_index("member")
    grid_index = lax.axis_index("grid")
    members = lax.axis_size("member")
    grid_count = lax.axis_size("grid")
    total = points * grid_count
    place = (grid_index * points + jnp.arange(points, dtype=jnp.int32)).astype(jnp.float32)
    area = jnp.cos(1.4 * (place + 0.5) / total)
    scale_map = area[None, :] * var_weight[:, None]
    partner_rows = lax.dynamic_index_in_dim(plan, member, 1, keepdims=False)
    pre = jnp.dot(hidden_in, w_full, preferred_element_type=jnp.float32) + b_in[None, :]
    act = jax.nn.gelu(pre).astype(jnp.bfloat16)
    field = jnp.dot(w_out, act.T, preferred_element_type=jnp.float32) + b_out[:, None]
    pre, act, field = (pre, act, field)
    fold_all = make_fold(field, partner_rows)
    slope_sum, spread_sum = fold_all(
        (
            jnp.zeros((w_out.shape[0], points), jnp.float32),
            jnp.zeros((w_out.shape[0], points), jnp.float32),
        ),
        lax.all_gather(field[None], "member", axis=0, tiled=True),
        jnp.int32(0),
    )
    miss = field - targets
    miss_root = jnp.sqrt(miss * miss + DELTA * DELTA)
    cot = scale_map * (miss / miss_root - slope_sum / rounds)
    terms = scale_map * (miss_root - DELTA - spread_sum / (2.0 * rounds))
    cot_b = cot.astype(jnp.bfloat16)
    dact = jnp.dot(cot_b.T, w_out, preferred_element_type=jnp.float32)
    _, pull = jax.vjp(jax.nn.gelu, pre)
    dpre = pull(dact)[0]
    dpre_b = dpre.astype(jnp.bfloat16)
    grad_hidden = jnp.dot(dpre_b, w_full.T, preferred_element_type=jnp.float32).astype(jnp.bfloat16)
    kappa = 4.0 / jnp.sqrt(jnp.float32(members * total))
    out_term = jnp.dot(cot_b, act, preferred_element_type=jnp.float32)
    sum_w2, sum_b2, sum_b1, sum_loss = lax.psum(
        (out_term, jnp.sum(cot, axis=1), jnp.sum(dpre, axis=0), jnp.sum(terms)), ("member", "grid")
    )
    row_count = w_in.shape[0]
    full_term = jnp.dot(hidden_in.T, dpre_b, preferred_element_type=jnp.float32)
    summed = lax.psum(full_term, ("member", "grid"))
    offset = (member * grid_count + grid_index) * row_count
    own_rows = lax.dynamic_slice_in_dim(summed, offset, row_count, 0)
    loss = sum_loss / (members * total * w_out.shape[0])
    return (
        loss,
        grad_hidden[None],
        own_rows * kappa,
        sum_b1 * kappa,
        sum_w2 * kappa,
        sum_b2 * kappa,
    )


def solution(mesh):
    placed = (
        P("member", "grid", None),
        P(("member", "grid"), None),
        P(),
        P(),
        P(),
        P(None, "grid"),
        P(),
        P(),
    )
    return jax.shard_map(
        shards,
        mesh=mesh,
        in_specs=placed,
        out_specs=(P(), P("member", "grid", None), P(("member", "grid"), None), P(), P(), P()),
        check_vma=False,
    )
```

profile of v0, /device:TPU:0, one launch (start us, length us, event | category | flops | bytes accessed | tf_op | source)
XLA Modules:
  0.0 314.8 jit_solution(176312685876041185)
XLA Ops:
  7.2 0.0 copy-start
  7.2 0.0 all-gather.5.cloned.1.call-start
  7.2 0.7 all-gather.5.cloned.1.call-update
  7.9 0.0 all-gather.7.cloned.1.call-start
  8.0 62.1 %all-gather.5.cloned.1.call-done = bf16[1024,1024]{1,0:T(8,128)(2,1)} async-done(((bf16[32,1024]{1,0:T(8,128)(2,1)}), bf16[1024,1024]{1,0:T(8,128)(2,1)}) %all-gather.5.cloned.1.call-update) | async-done | bytes 2097168 | tf_op jit(solution)/shard_map/all_gather | solution.py:28
  70.1 12.6 %multiply_convert_fusion = (bf16[2048,1024]{1,0:T(8,128)(2,1)S(1)}, f32[2048,1024]{1,0:T(8,128)}) fusion(f32[1024]{0:T(1024)} %param.10, bf16[1024,1024]{1,0:T(8,128)(2,1)} %all-gather.5.cloned.1.call-done, bf16[1,2048,1024]{2,1,0:T(8,128)(2,1)} %param.8), kind=kOutput, calls=%fused_computation.8 | convolution fusion | flops 4315938816 | bytes 18878464 | tf_op jit(solution)/shard_map/dot_general | solution.py:38
  82.7 2.0 copy-done.1
  84.8 2.4 convolution_add_fusion
  87.1 0.0 all-gather.7.cloned.1.call-update
  87.1 0.2 all-reduce.4.cloned.1.call-start
  87.4 0.2 dynamic-slice_reduce_fusion
  87.6 0.1 multiply_cosine_fusion
  87.6 0.1 convert_reduce_fusion
  87.7 44.5 %all-gather.7.cloned.1.call-done = f32[4,100,2048]{2,1,0:T(8,128)} async-done(((f32[1,100,2048]{2,1,0:T(8,128)}), f32[4,100,2048]{2,1,0:T(8,128)}) %all-gather.7.cloned.1.call-update) | async-done | bytes 3276816 | tf_op jit(solution)/shard_map/all_gather | solution.py:48
  132.2 4.1 %fusion.10 = (bf16[4,100,2048]{2,1,0:T(8,128)(2,1)S(1)}, bf16[4,100,2048]{2,1,0:T(8,128)(2,1)S(1)}) fusion(f32[4,100,2048]{2,1,0:T(8,128)} %all-gather.7.cloned.1.call-done, f32[100,2048]{1,0:T(8,128)} %bitcast.49), kind=kLoop, calls=%fused_computation.15 | loop fusion | flops 5734400 | bytes 7372800 | tf_op jit(solution)/shard_map/div | solution.py:17
  136.3 0.0 copy-start.7
  136.3 1.3 fusion.12
  137.7 1.3 fusion.14
  139.1 1.9 fusion.29
  140.9 1.6 fusion.24
  142.5 7.0 %fusion.30 = (f32[1024]{0:T(1024)S(1)}, bf16[2048,1024]{1,0:T(8,128)(2,1)S(1)}) fusion(f32[2048,1024]{1,0:T(8,128)S(1)} %bitcast.51, f32[1024]{0:T(1024)S(1)} %copy-done.10, bf16[100,1024]{1,0:T(8,128)(2,1)S(1)} %copy-done, bf16[100,2048]{1,0:T(8,128)(2,1)S(1)} %get-tuple-element.30), kind=kOutput, calls=%fused_computation.47 | convolution fusion | flops 465566720 | bytes 13205504 | tf_op jit(solution)/shard_map/dot_general | solution.py:56
  149.5 2.0 copy-done.11
  151.5 6.2 %fusion.16 = f32[1024,1024]{0,1:T(8,128)} fusion(bf16[1,2048,1024]{2,1,0:T(8,128)(2,1)S(1)} %copy-done.8, bf16[2048,1024]{1,0:T(8,128)(2,1)S(1)} %get-tuple-element.37), kind=kOutput, calls=%fused_computation.22 | convolution fusion | flops 4294967296 | bytes 12582912 | tf_op jit(solution)/shard_map/dot_general | solution.py:67
  157.7 0.0 all-reduce.4.cloned.1.call-update
  157.7 40.3 %all-reduce = (f32[]{:T(128)}, f32[1024]{0:T(1024)S(1)}, f32[100]{0:T(128)S(1)}) all-reduce(f32[]{:T(128)} %get-tuple-element.33, f32[1024]{0:T(1024)S(1)} %get-tuple-element.36, f32[100]{0:T(128)S(1)} %get-tuple-element.29), channel_id=1, replica_groups=mesh['member'=4,'grid'=8] {'member','grid'}, use_global_device_ids=true, to_apply=%region_2.3 | all-reduce | flops 1125 | bytes 9000 | tf_op jit(solution)/shard_map/psum | solution.py:63
  198.7 0.5 broadcast_multiply_fusion.2
  199.2 0.6 broadcast_multiply_fusion.1
  199.8 8.3 %convert_bitcast_fusion = bf16[1,2048,1024]{2,1,0:T(8,128)(2,1)} fusion(bf16[1024,1024]{1,0:T(8,128)(2,1)S(1)} %copy-done.9, bf16[2048,1024]{1,0:T(8,128)(2,1)} %copy-done.11), kind=kOutput, calls=%fused_computation.13 | convolution fusion | flops 4297064448 | bytes 10485760 | tf_op jit(solution)/shard_map/dot_general | solution.py:60
  208.1 95.1 %all-reduce.4.cloned.1.call-done = (f32[1024,1024]{0,1:T(8,128)}, f32[100,1024]{1,0:T(8,128)}) async-done(((f32[1024,1024]{0,1:T(8,128)}, f32[100,1024]{1,0:T(8,128)}), (f32[1024,1024]{0,1:T(8,128)}, f32[100,1024]{1,0:T(8,128)})) %all-reduce.4.cloned.1.call-update) | async-done | bytes 4603920 | tf_op jit(solution)/shard_map/psum | solution.py:68
  303.2 1.2 dynamic-slice_multiply_fusion
  304.5 0.8 copy.16
  305.3 1.8 broadcast_multiply_fusion
  (25 shorter events, 0.1 us)
Async XLA Ops:
  7.2 77.6 %copy-start = (bf16[100,1024]{1,0:T(8,128)(2,1)S(1)}, bf16[100,1024]{1,0:T(8,128)(2,1)}, u32[]{:S(2)}) copy-start(bf16[100,1024]{1,0:T(8,128)(2,1)} %param.11) | copy-start | bytes 614404
  7.2 62.9 %all-gather.5.cloned.1.call-start = ((), (), s32[]{:S(2)}) async-start(), calls=%async_computation | async-start | bytes 2162688 | tf_op jit(solution)/shard_map/all_gather | solution.py:28
  7.9 76.8 %copy-start.5 = (f32[100]{0:T(128)S(1)}, f32[100]{0:T(128)}, u32[]{:S(2)}) copy-start(f32[100]{0:T(128)} %param.12) | copy-start | bytes 1204
  7.9 124.3 %all-gather.7.cloned.1.call-start = ((), (), s32[]{:S(2)}) async-start(), calls=%async_computation.1 | async-start | bytes 4259840 | tf_op jit(solution)/shard_map/all_gather | solution.py:48
  82.7 2.0 copy-start.1
  82.7 4.6 %copy-start.6 = (s32[3,4]{1,0:T(4,128)S(1)}, s32[3,4]{1,0:T(4,128)}, u32[]{:S(2)}) copy-start(s32[3,4]{1,0:T(4,128)} %param.15) | copy-start | bytes 148
  87.1 216.1 %all-reduce.4.cloned.1.call-start = ((), (), s32[]{:S(2)}) async-start(), calls=%async_computation.2 | async-start | bytes 9240576 | tf_op jit(solution)/shard_map/psum | solution.py:68
  132.2 10.3 %slice-start = ((s8[8388608]{0:T(1024)(128)(4,1)}), s8[4194304]{0:T(1024)(128)(4,1)S(1)}, s32[]{:S(2)}) async-start(s8[8388608]{0:T(1024)(128)(4,1)} %bitcast.50), calls=%async_computation.3 | async-start | bytes 8388608
  136.3 2.7 copy-start.3
  136.3 2.7 copy-start.4
  136.3 2.7 copy-start.7
  137.7 3.3 %copy-start.2 = (bf16[2048,1024]{1,0:T(8,128)(2,1)S(1)}, bf16[2048,1024]{1,0:T(8,128)(2,1)}, u32[]{:S(2)}) copy-start(bf16[2048,1024]{1,0:T(8,128)(2,1)} %copy-done.1) | copy-start | bytes 12582916
  137.7 4.8 %slice-start.1 = ((s8[8388608]{0:T(1024)(128)(4,1)}), s8[4194304]{0:T(1024)(128)(4,1)S(1)}, s32[]{:S(2)}) async-start(s8[8388608]{0:T(1024)(128)(4,1)} %bitcast.50), calls=%async_computation.4 | async-start | bytes 8388608
  139.0 3.4 %copy-start.10 = (f32[1024]{0:T(1024)S(1)}, f32[1024]{0:T(1024)}, u32[]{:S(2)}) copy-start(f32[1024]{0:T(1024)} %param.10) | copy-start | bytes 12292
  142.5 9.0 %copy-start.8 = (bf16[1,2048,1024]{2,1,0:T(8,128)(2,1)S(1)}, bf16[1,2048,1024]{2,1,0:T(8,128)(2,1)}, u32[]{:S(2)}) copy-start(bf16[1,2048,1024]{2,1,0:T(8,128)(2,1)} %param.8) | copy-start | bytes 12582916
  149.5 2.0 copy-start.11
  157.7 42.1 %copy-start.9 = (bf16[1024,1024]{1,0:T(8,128)(2,1)S(1)}, bf16[1024,1024]{1,0:T(8,128)(2,1)}, u32[]{:S(2)}) copy-start(bf16[1024,1024]{1,0:T(8,128)(2,1)} %all-gather.5.cloned.1.call-done) | copy-start | bytes 6291460
Sparse Core Ops, SparseCore 0:
  11.0 59.0 all-gather.4
  87.3 44.8 all-gather.6
  157.8 145.3 all-reduce.3
where the time goes:
time: 315 us
  waiting for transfers between devices  202 us (64%)
  matrix products  40.7 us (13%)
  blocking collectives  40.3 us (13%)
  between operations  15.7 us (5%)
  other arithmetic  10.2 us (3%)
  local copies, waits for them, and re-layouts  5.12 us (2%)
    psum x1, waiting for transfers between devices, shards(): summed = lax.psum(full_term, ('member', 'grid'))  95.1 us
    all_gather x1, waiting for transfers between devices, shards(): w_full = lax.all_gather(w_in, ('member', 'grid'), axis=0, tiled=True)  62.1 us
    all_gather x1, waiting for transfers between devices, shards(): lax.all_gather(field[None], 'member', axis=0, tiled=True)  44.5 us
    psum x1, blocking collectives, shards(): lax.psum((out_term, jnp.sum(cot, axis=1), jnp.sum(dpre, axis=0), jnp.sum(...  40.3 us
    dot_general x1, matrix products, shards(): jnp.dot(hidden_in, w_full, preferred_element_type=jnp.float32)  12.6 us
    dot_general x1, matrix products, shards(): jnp.dot(dpre_b, w_full.T, preferred_element_type=jnp.float32)  8.35 us
    dot_general x1, matrix products, shards(): dact = jnp.dot(cot_b.T, w_out, preferred_element_type=jnp.float32)  6.99 us
  transfers between devices with their start and end apart: 3, of which 3 were waited for; matrix products, arithmetic and copies ran while one was open for 3% of the time, Pallas kernels for 0%

commit v1 on v0

--- a/solution.py
+++ b/solution.py
@@ -61,7 +61,8 @@
     kappa = 4.0 / jnp.sqrt(jnp.float32(members * total))
     out_term = jnp.dot(cot_b, act, preferred_element_type=jnp.float32)
     sum_w2, sum_b2, sum_b1, sum_loss = lax.psum(
-        (out_term, jnp.sum(cot, axis=1), jnp.sum(dpre, axis=0), jnp.sum(terms)), ("member", "grid")
+        lax.psum((out_term, jnp.sum(cot, axis=1), jnp.sum(dpre, axis=0), jnp.sum(terms)), "grid"),
+        "member",
     )
     row_count = w_in.shape[0]
     full_term = jnp.dot(hidden_in.T, dpre_b, preferred_element_type=jnp.float32)

time: 315 us -> 403 us (1.28)
  waiting for transfers between devices: 202 us -> 299 us
  blocking collectives: 40.3 us -> 27 us
  matrix products: 40.7 us -> 47.5 us
    psum x1, waiting for transfers between devices: 95.1 us -> 146 us  [shards(): summed = lax.psum(full_term, ('member', 'grid'))]
    psum x0 -> x2, waiting for transfers between devices: none -> 45.2 us  [the longest x1 44.6 us: shards(): lax.psum((out_term, jnp.sum(cot, axis=1), jnp.sum(dpre, axis=0), jnp.sum(...]
    psum x1, blocking collectives: 40.3 us -> 16.2 us  [shards(): lax.psum((out_term, jnp.sum(cot, axis=1), jnp.sum(dpre, axis=0), jnp.sum(...]
    psum x0 -> x1, blocking collectives: none -> 10.8 us  [shards(): lax.psum(lax.psum((out_term, jnp.sum(cot, axis=1), jnp.sum(dpre, axis=0),...]
  transfers between devices with their start and end apart: 3 -> 5, of which waited for: 3 -> 5; matrix products, arithmetic and copies ran while one was open for 3% -> 8% of each run, Pallas kernels for 0% -> 0%
where the time goes in v1:
time: 403 us
  waiting for transfers between devices  299 us (74%)
  matrix products  47.5 us (12%)
  blocking collectives  27 us (7%)
  between operations  15.7 us (4%)
  other arithmetic  10.1 us (3%)
    psum x1, waiting for transfers between devices, shards(): summed = lax.psum(full_term, ('member', 'grid'))  146 us
    all_gather x1, waiting for transfers between devices, shards(): w_full = lax.all_gather(w_in, ('member', 'grid'), axis=0, tiled=True)  62.1 us
    psum x1, waiting for transfers between devices, shards(): lax.psum((out_term, jnp.sum(cot, axis=1), jnp.sum(dpre, axis=0), jnp.sum(...  44.6 us
    all_gather x1, waiting for transfers between devices, shards(): lax.all_gather(field[None], 'member', axis=0, tiled=True)  44.5 us
    psum x1, blocking collectives, shards(): lax.psum((out_term, jnp.sum(cot, axis=1), jnp.sum(dpre, axis=0), jnp.sum(...  16.2 us
    dot_general x1, matrix products, shards(): jnp.dot(hidden_in, w_full, preferred_element_type=jnp.float32)  12.5 us
    psum x1, blocking collectives, shards(): lax.psum(lax.psum((out_term, jnp.sum(cot, axis=1), jnp.sum(dpre, axis=0),...  10.8 us
    dot_general x1, matrix products, shards(): dact = jnp.dot(cot_b.T, w_out, preferred_element_type=jnp.float32)  10.1 us
  transfers between devices with their start and end apart: 5, of which 5 were waited for; matrix products, arithmetic and copies ran while one was open for 8% of the time, Pallas kernels for 0%

profile of v1, /device:TPU:0, one launch (start us, length us, event | category | flops | bytes accessed | tf_op | source)
XLA Modules:
  0.0 402.7 jit_solution(18315557388715117522)
XLA Ops:
  7.2 0.0 all-gather.5.cloned.1.call-start
  7.2 0.7 all-gather.5.cloned.1.call-update
  7.9 0.0 all-gather.7.cloned.1.call-start
  8.0 62.1 %all-gather.5.cloned.1.call-done = bf16[1024,1024]{1,0:T(8,128)(2,1)} async-done(((bf16[32,1024]{1,0:T(8,128)(2,1)}), bf16[1024,1024]{1,0:T(8,128)(2,1)}) %all-gather.5.cloned.1.call-update) | async-done | bytes 2097168 | tf_op jit(solution)/shard_map/all_gather | solution.py:28
  70.1 12.5 %multiply_convert_fusion = (bf16[2048,1024]{1,0:T(8,128)(2,1)S(1)}, f32[2048,1024]{1,0:T(8,128)}) fusion(f32[1024]{0:T(1024)} %param.10, bf16[1024,1024]{1,0:T(8,128)(2,1)} %all-gather.5.cloned.1.call-done, bf16[1,2048,1024]{2,1,0:T(8,128)(2,1)} %param.8), kind=kOutput, calls=%fused_computation.8 | convolution fusion | flops 4315938816 | bytes 18878464 | tf_op jit(solution)/shard_map/dot_general | solution.py:38
  82.6 2.0 copy-done.1
  84.6 2.4 convolution_add_fusion
  87.0 0.2 all-reduce.8.cloned.1.call-start
  87.2 0.2 dynamic-slice_reduce_fusion
  87.4 0.1 multiply_cosine_fusion
  87.5 0.1 convert_reduce_fusion
  87.6 44.5 %all-gather.7.cloned.1.call-done = f32[4,100,2048]{2,1,0:T(8,128)} async-done(((f32[1,100,2048]{2,1,0:T(8,128)}), f32[4,100,2048]{2,1,0:T(8,128)}) %all-gather.7.cloned.1.call-update) | async-done | bytes 3276816 | tf_op jit(solution)/shard_map/all_gather | solution.py:48
  132.0 3.9 fusion.10
  136.0 1.3 fusion.12
  137.4 1.3 fusion.14
  138.8 1.9 fusion.29
  140.6 1.6 fusion.24
  142.2 0.0 all-reduce.10.cloned.1.call-start
  142.3 10.1 %fusion.30 = (f32[1024]{0:T(1024)S(1)}, bf16[2048,1024]{1,0:T(8,128)(2,1)}) fusion(f32[2048,1024]{1,0:T(8,128)} %get-tuple-element.36, f32[1024]{0:T(1024)S(1)} %copy-done.9, bf16[100,1024]{1,0:T(8,128)(2,1)S(1)} %copy-done, bf16[100,2048]{1,0:T(8,128)(2,1)S(1)} %get-tuple-element.31), kind=kOutput, calls=%fused_computation.47 | convolution fusion | flops 465566720 | bytes 13205504 | tf_op jit(solution)/shard_map/dot_general | solution.py:56
  152.4 44.6 %all-reduce.8.cloned.1.call-done = f32[100,1024]{1,0:T(8,128)} async-done(((f32[100,1024]{1,0:T(8,128)}), f32[100,1024]{1,0:T(8,128)}) %all-reduce.8.cloned.1.call-update) | async-done | bytes 409616 | tf_op jit(solution)/shard_map/psum | solution.py:64
  197.0 0.3 all-reduce.6.cloned.1.call-start
  197.2 10.0 %fusion.16 = f32[1024,1024]{0,1:T(8,128)} fusion(bf16[1,2048,1024]{2,1,0:T(8,128)(2,1)} %param.8, bf16[2048,1024]{1,0:T(8,128)(2,1)} %get-tuple-element.38), kind=kOutput, calls=%fused_computation.22 | convolution fusion | flops 4294967296 | bytes 12582912 | tf_op jit(solution)/shard_map/dot_general | solution.py:68
  207.3 16.2 %all-reduce = (f32[]{:T(128)}, f32[1024]{0:T(1024)S(1)}, f32[100]{0:T(128)S(1)}) all-reduce(f32[]{:T(128)} %get-tuple-element.34, f32[1024]{0:T(1024)S(1)} %get-tuple-element.37, f32[100]{0:T(128)S(1)} %get-tuple-element.30), channel_id=1, replica_groups=mesh['member'=4,'grid'=8] {'grid'}, use_global_device_ids=true, to_apply=%region_2.3 | all-reduce | flops 1125 | bytes 9000 | tf_op jit(solution)/shard_map/psum | solution.py:64
  223.4 10.8 %all-reduce.1 = (f32[]{:T(128)}, f32[1024]{0:T(1024)S(1)}, f32[100]{0:T(128)S(1)}) all-reduce(f32[]{:T(128)} %get-tuple-element.24, f32[1024]{0:T(1024)S(1)} %get-tuple-element.25, f32[100]{0:T(128)S(1)} %get-tuple-element.26), channel_id=1, replica_groups=mesh['member'=4,'grid'=8] {'member'}, use_global_device_ids=true, to_apply=%region_3.4 | all-reduce | flops 1125 | bytes 9000 | tf_op jit(solution)/shard_map/psum | solution.py:63
  234.9 0.5 broadcast_multiply_fusion.2
  235.5 0.6 broadcast_multiply_fusion.1
  236.1 8.3 %convert_bitcast_fusion = bf16[1,2048,1024]{2,1,0:T(8,128)(2,1)} fusion(bf16[1024,1024]{1,0:T(8,128)(2,1)S(1)} %copy-done.8, bf16[2048,1024]{1,0:T(8,128)(2,1)} %get-tuple-element.38), kind=kOutput, calls=%fused_computation.13 | convolution fusion | flops 4297064448 | bytes 10485760 | tf_op jit(solution)/shard_map/dot_general | solution.py:60
  244.4 0.6 all-reduce.10.cloned.1.call-done
  245.0 1.8 broadcast_multiply_fusion
  246.8 146.1 %all-reduce.6.cloned.1.call-done = f32[1024,1024]{0,1:T(8,128)} async-done(((f32[1024,1024]{0,1:T(8,128)}), f32[1024,1024]{0,1:T(8,128)}) %all-reduce.6.cloned.1.call-update) | async-done | bytes 4194320 | tf_op jit(solution)/shard_map/psum | solution.py:69
  392.9 1.2 dynamic-slice_multiply_fusion
  394.2 0.8 copy.16
  (23 shorter events, 0.1 us)
Async XLA Ops:
  7.2 77.4 %copy-start = (bf16[100,1024]{1,0:T(8,128)(2,1)S(1)}, bf16[100,1024]{1,0:T(8,128)(2,1)}, u32[]{:S(2)}) copy-start(bf16[100,1024]{1,0:T(8,128)(2,1)} %param.11) | copy-start | bytes 614404
  7.2 62.9 %all-gather.5.cloned.1.call-start = ((), (), s32[]{:S(2)}) async-start(), calls=%async_computation | async-start | bytes 2162688 | tf_op jit(solution)/shard_map/all_gather | solution.py:28
  7.9 76.7 %copy-start.5 = (f32[100]{0:T(128)S(1)}, f32[100]{0:T(128)}, u32[]{:S(2)}) copy-start(f32[100]{0:T(128)} %param.12) | copy-start | bytes 1204
  7.9 124.1 %all-gather.7.cloned.1.call-start = ((), (), s32[]{:S(2)}) async-start(), calls=%async_computation.4 | async-start | bytes 4259840 | tf_op jit(solution)/shard_map/all_gather | solution.py:48
  82.6 2.0 copy-start.1
  82.6 4.6 %copy-start.6 = (s32[3,4]{1,0:T(4,128)S(1)}, s32[3,4]{1,0:T(4,128)}, u32[]{:S(2)}) copy-start(s32[3,4]{1,0:T(4,128)} %param.15) | copy-start | bytes 148
  87.0 109.9 %all-reduce.8.cloned.1.call-start = ((), (), s32[]{:S(2)}) async-start(), calls=%async_computation.2 | async-start | bytes 851968 | tf_op jit(solution)/shard_map/psum | solution.py:64
  136.0 2.7 copy-start.3
  136.0 2.7 copy-start.4
  136.0 2.7 copy-start.7
  137.4 3.3 copy-start.2
  138.7 3.5 copy-start.9
  142.2 102.8 %all-reduce.10.cloned.1.call-start = ((), (), s32[]{:S(2)}) async-start(), calls=%async_computation.3 | async-start | bytes 851968 | tf_op jit(solution)/shard_map/psum | solution.py:63
  197.0 196.0 %all-reduce.6.cloned.1.call-start = ((), (), s32[]{:S(2)}) async-start(), calls=%async_computation.1 | async-start | bytes 8388608 | tf_op jit(solution)/shard_map/psum | solution.py:69
  207.2 28.8 %copy-start.8 = (bf16[1024,1024]{1,0:T(8,128)(2,1)S(1)}, bf16[1024,1024]{1,0:T(8,128)(2,1)}, u32[]{:S(2)}) copy-start(bf16[1024,1024]{1,0:T(8,128)(2,1)} %all-gather.5.cloned.1.call-done) | copy-start | bytes 6291460
Sparse Core Ops, SparseCore 0:
  11.0 59.0 all-gather.4
  87.1 44.8 all-gather.6
  142.3 54.5 all-reduce.7
  199.8 45.1 all-reduce.9
  250.4 142.4 all-reduce.5
